TPU v7x, 512 devices: a whole 4x4x16 slice. The times are simulated.
512 devices in a mesh: dom: 128 (over y, z, core), field: 4 (over x).
Axes of the slice: x: 4, y: 4, z: 16, core: 2. Of those that a mesh axis runs over, the one named last changes fastest.
Arguments:
- adjoint: bfloat16 [1024, 384, 128], P('dom', 'field'), may hold values from -6 to 6
- face_blocks: bfloat16 [4480, 384, 384], P('dom', 'field'), may hold values from -0.3125 to 0.3125
- diag_blocks: bfloat16 [1024, 384, 384], P('dom', 'field'), may hold values from -0.3125 to 0.3125
- face_left: int32 [4480], P('dom'), may hold values from 0 to 7
- face_right: int32 [4480], P('dom'), may hold values from 0 to 7
- face_code: int32 [4480], P('dom'), may hold values from 0 to 7
- side_counts: int32 [128, 5], P('dom'), may hold values from 1 to 7, 24 in all within a row
Outputs:
- psi: bfloat16 [1024, 384, 128], P('dom', 'field')
- second: bfloat16 [1024, 384, 128], P('dom', 'field')
Inputs may be any that keep to these rules, and one draw needn't show every extreme that they name: `side_counts`: the 5 lists of one partition hold 24 live faces together, each list at least one, and some list of every partition is full with 7. `face_right`: slots at or beyond a list's count are unused; their indices and blocks are arbitrary.
All inputs are finite; a program needn't handle non-finite values.
Results may differ from a plain program's by a relative error of at most 0.0049.
Values may be sent and summed in bfloat16 or wider, within the bound.
No kernel may reach another device: no remote copies, remote signals or barrier semaphores. Data moves between devices by JAX's collectives and lax.ppermute only.
A program may use at most 64 MiB of HBM per device.

v0:
```python
import jax
import jax.numpy as jnp
from jax import lax
from jax.sharding import PartitionSpec as P

PTS = 4
NS = 5


def from_behind(array, axis, by):
    peers = lax.axis_size(axis)
    return lax.ppermute(array, axis, [(i, (i + by) % peers) for i in range(peers)])


def orient(blocks, orient_code):
    number = blocks.shape[0]
    shaped = blocks.reshape(number, blocks.shape[1] // (PTS * PTS), PTS, PTS, blocks.shape[2])
    flip_rows = (orient_code % 2 == 1)[:, None, None, None, None]
    flip_cols = (orient_code // 2 % 2 == 1)[:, None, None, None, None]
    swap_both = (orient_code >= 4)[:, None, None, None, None]
    shaped = jnp.where(flip_rows, jnp.flip(shaped, 2), shaped)
    shaped = jnp.where(flip_cols, jnp.flip(shaped, 3), shaped)
    shaped = jnp.where(swap_both, jnp.swapaxes(shaped, 2, 3), shaped)
    return shaped.reshape(blocks.shape)


def deposit(summed, product, targets):
    n_elems = summed.shape[0]
    onehot = (targets[None, :] == jnp.arange(n_elems, dtype=jnp.int32)[:, None]).astype(jnp.float32)
    return summed + jnp.einsum("ec,cxk->exk", onehot, product, precision=lax.Precision.HIGHEST)


def local(adjoint, face_blocks, diag_blocks, face_left, face_right, face_code, side_counts):
    n_domains = lax.axis_size("dom")
    stride = n_domains // 8
    offsets = [0, 1, -1, stride, -stride]
    capacity = face_blocks.shape[0] // NS
    slot_index = jnp.arange(capacity, dtype=jnp.int32)
    live_flags = (slot_index[None, :] < side_counts[0][:, None]).reshape(NS * capacity)
    oriented = orient(face_blocks, face_code)
    prepared = jnp.where(live_flags[:, None, None], oriented, jnp.zeros_like(oriented))
    targets = face_right.reshape(NS, capacity)
    sources = face_left.reshape(NS, capacity)
    target_list = [targets[0]]
    for side in range(1, NS):
        target_list.append(from_behind(targets[side], "dom", offsets[side]))
    all_targets = jnp.concatenate(target_list, 0)
    block_sides = prepared.reshape(NS, capacity, prepared.shape[1], prepared.shape[2])
    moved = [block_sides[0]]
    for side in range(1, NS):
        moved.append(from_behind(block_sides[side], "dom", offsets[side]))
    all_blocks = jnp.concatenate(moved, 0)

    def apply_op(vector):
        whole = lax.all_gather(vector, "field", axis=1, tiled=True)
        summed = jnp.einsum("ecr,erk->eck", diag_blocks, whole, preferred_element_type=jnp.float32)
        row_list = [jnp.take(whole, sources[0], axis=0)]
        for side in range(1, NS):
            halo_rows = jnp.take(vector, sources[side], axis=0)
            landed = from_behind(halo_rows, "dom", offsets[side])
            row_list.append(lax.all_gather(landed, "field", axis=1, tiled=True))
        rows_all = jnp.concatenate(row_list, 0)
        product = jnp.einsum(
            "scr,srk->sck", all_blocks, rows_all, preferred_element_type=jnp.float32
        )
        return deposit(summed, product, all_targets)

    first = apply_op(adjoint)
    psi = (adjoint.astype(jnp.float32) - 0.5 * first).astype(jnp.bfloat16)
    second = apply_op(psi).astype(jnp.bfloat16)
    return (psi, second)


def solution(mesh):
    return jax.shard_map(
        local,
        mesh=mesh,
        in_specs=(
            P("dom", "field", None),
            P("dom", "field", None),
            P("dom", "field", None),
            P("dom"),
            P("dom"),
            P("dom"),
            P("dom", None),
        ),
        out_specs=(P("dom", "field", None), P("dom", "field", None)),
        check_vma=False,
    )
```

profile of v0, /device:TPU:466, one launch (start us, length us, event | category | flops | bytes accessed | tf_op | source)
XLA Modules:
  0.0 374.7 jit_solution(1725992629330623298)
XLA Ops:
  0.7 4.4 %reshape.72 = bf16[35,6,4,4,384]{4,3,2,1,0:T(4,128)(2,1)S(1)} reshape(bf16[35,96,384]{2,1,0:T(8,128)(2,1)} %param.12) | data formatting | bytes 5160960 | tf_op jit(solution)/shard_map/reshape | solution.py:17
  5.1 3.2 reverse_select_fusion
  8.3 15.0 %rev.9 = bf16[35,6,4,4,384]{4,3,2,1,0:T(4,128)(2,1)} reverse(bf16[35,6,4,4,384]{4,3,2,1,0:T(4,128)(2,1)} %reverse_select_fusion), dimensions={3} | reverse | bytes 5160960 | tf_op jit(solution)/shard_map/jit(_flip)/rev | solution.py:22
  23.3 5.2 %broadcast_select_fusion = bf16[35,6,4,4,384]{4,3,2,1,0:T(4,128)(2,1)S(1)} fusion(bf16[35,6,4,4,384]{4,3,2,1,0:T(4,128)(2,1)} %rev.9, pred[35]{0:T(512)(128)(4,1)S(1)} %get-tuple-element.34, bf16[35,6,4,4,384]{4,3,2,1,0:T(4,128)(2,1)S(1)} %reshape.72, pred[35]{0:T(512)(128)(4,1)S(1)} %get-tuple-element.33), kind=kLoop, calls=%fused_computation.12 | loop fusion | flops 2580480 | bytes 7741510 | tf_op jit(solution)/shard_map/jit(_where)/select_n | solution.py:22
  28.5 3.1 bitcast_select_fusion
  31.5 4.1 %reshape.73 = bf16[35,96,384]{2,1,0:T(8,128)(2,1)S(1)} reshape(bf16[35,6,4,4,384]{4,3,2,1,0:T(4,128)(2,1)} %bitcast_select_fusion) | data formatting | bytes 5160960 | tf_op jit(solution)/shard_map/reshape | solution.py:24
  39.6 3.6 collective-permute-start.5
  43.2 6.2 %collective-permute-start.6 = (bf16[7,96,384]{2,1,0:T(8,128)(2,1)}, bf16[7,96,384]{2,1,0:T(8,128)(2,1)}, u32[]{:S(2)}, u32[]{:S(2)}) collective-permute-start(bf16[7,96,384]{2,1,0:T(8,128)(2,1)} %get-tuple-element.15), channel_id=1, source_target_pairs={{0,64},{4,68},{8,72},{12,76},{16,80},{20,84},{24,88},{28,92},{32,9... | collective-permute-start | bytes 1548296 | tf_op jit(solution)/shard_map/ppermute | solution.py:12
  54.0 3.9 %collective-permute-start = (s32[7]{0:T(128)}, s32[7]{0:T(128)}, u32[]{:S(2)}, u32[]{:S(2)}) collective-permute-start(s32[7]{0:T(128)} %get-tuple-element.21), channel_id=1, source_target_pairs={{0,4},{4,8},{8,12},{12,16},{16,20},{20,24},{24,28},{28,32},{32,36}... | collective-permute-start | bytes 92 | tf_op jit(solution)/shard_map/ppermute | solution.py:12
  57.9 15.1 %all_gather.30 = bf16[8,384,128]{2,1,0:T(8,128)(2,1)} all-gather(bf16[8,96,128]{2,1,0:T(8,128)(2,1)S(1)} %copy-done.3), channel_id=1, replica_groups=mesh['dom'=128,'field'=4] {'field'}, dimensions={1}, use_global_device_ids=true | all-gather | bytes 983040 | tf_op jit(solution)/shard_map/all_gather | solution.py:55
  92.6 5.7 %collective-permute-done.1 = s32[7]{0:T(128)} collective-permute-done((s32[7]{0:T(128)}, s32[7]{0:T(128)}, u32[]{:S(2)}, u32[]{:S(2)}) %collective-permute-start.1) | collective-permute-done | bytes 60 | tf_op jit(solution)/shard_map/ppermute | solution.py:12
  98.3 8.8 %collective-permute-start.2 = (s32[7]{0:T(128)}, s32[7]{0:T(128)}, u32[]{:S(2)}, u32[]{:S(2)}) collective-permute-start(s32[7]{0:T(128)} %get-tuple-element.23), channel_id=1, source_target_pairs={{0,64},{4,68},{8,72},{12,76},{16,80},{20,84},{24,88},{28,92},{32,9... | collective-permute-start | bytes 92 | tf_op jit(solution)/shard_map/ppermute | solution.py:12
  107.1 5.4 %collective-permute-done.2 = s32[7]{0:T(128)} collective-permute-done((s32[7]{0:T(128)}, s32[7]{0:T(128)}, u32[]{:S(2)}, u32[]{:S(2)}) %collective-permute-start.2) | collective-permute-done | bytes 60 | tf_op jit(solution)/shard_map/ppermute | solution.py:12
  112.5 9.0 %collective-permute-start.3 = (s32[7]{0:T(128)}, s32[7]{0:T(128)}, u32[]{:S(2)}, u32[]{:S(2)}) collective-permute-start(s32[7]{0:T(128)} %get-tuple-element.19), channel_id=1, source_target_pairs={{0,448},{4,452},{8,456},{12,460},{16,464},{20,468},{24,472},{28,47... | collective-permute-start | bytes 92 | tf_op jit(solution)/shard_map/ppermute | solution.py:12
  121.5 6.2 %collective-permute-done.3 = s32[7]{0:T(128)} collective-permute-done((s32[7]{0:T(128)}, s32[7]{0:T(128)}, u32[]{:S(2)}, u32[]{:S(2)}) %collective-permute-start.3) | collective-permute-done | bytes 60 | tf_op jit(solution)/shard_map/ppermute | solution.py:12
  127.7 8.1 %collective-permute-start.7 = (bf16[7,96,384]{2,1,0:T(8,128)(2,1)}, bf16[7,96,384]{2,1,0:T(8,128)(2,1)}, u32[]{:S(2)}, u32[]{:S(2)}) collective-permute-start(bf16[7,96,384]{2,1,0:T(8,128)(2,1)} %get-tuple-element.14), channel_id=1, source_target_pairs={{0,448},{4,452},{8,456},{12,460},{16,464},{20,468},{24,472},{28,47... | collective-permute-start | bytes 1548296 | tf_op jit(solution)/shard_map/ppermute | solution.py:12
  139.1 14.2 %all_gather.31 = bf16[7,384,128]{2,1,0:T(8,128)(2,1)S(1)} all-gather(bf16[7,96,128]{2,1,0:T(8,128)(2,1)} %collective-permute-done.8), channel_id=1, replica_groups=mesh['dom'=128,'field'=4] {'field'}, dimensions={1}, use_global_device_ids=true | all-gather | bytes 860160 | tf_op jit(solution)/shard_map/all_gather | solution.py:61
  153.3 35.4 %collective-permute-done.9 = bf16[7,96,128]{2,1,0:T(8,128)(2,1)S(1)} collective-permute-done((bf16[7,96,128]{2,1,0:T(8,128)(2,1)}, bf16[7,96,128]{2,1,0:T(8,128)(2,1)S(1)}, u32[]{:S(2)}, u32[]{:S(2)}) %collective-permute-start.9) | collective-permute-done | bytes 172064 | tf_op jit(solution)/shard_map/ppermute | solution.py:12
  190.7 14.3 %all_gather.32 = bf16[7,384,128]{2,1,0:T(8,128)(2,1)S(1)} all-gather(bf16[7,96,128]{2,1,0:T(8,128)(2,1)S(1)} %collective-permute-done.9), channel_id=1, replica_groups=mesh['dom'=128,'field'=4] {'field'}, dimensions={1}, use_global_device_ids=true | all-gather | bytes 860160 | tf_op jit(solution)/shard_map/all_gather | solution.py:61
  204.9 3.1 collective-permute-done.10
  208.0 9.5 %collective-permute-start.11 = (bf16[7,96,128]{2,1,0:T(8,128)(2,1)S(1)}, bf16[7,96,128]{2,1,0:T(8,128)(2,1)S(1)}, u32[]{:S(2)}, u32[]{:S(2)}) collective-permute-start(bf16[7,96,128]{2,1,0:T(8,128)(2,1)S(1)} %broadcast_select_fusion.3), channel_id=1, source_target_pairs={{0,448},{4,452},{8,456},{12,460},{16,464},{20,468},{24,472},{28,47... | collective-permute-start | bytes 516104 | tf_op jit(solution)/shard_map/ppermute | solution.py:12
  217.5 13.1 %all_gather.33 = bf16[7,384,128]{2,1,0:T(8,128)(2,1)S(1)} all-gather(bf16[7,96,128]{2,1,0:T(8,128)(2,1)S(1)} %collective-permute-done.10), channel_id=1, replica_groups=mesh['dom'=128,'field'=4] {'field'}, dimensions={1}, use_global_device_ids=true | all-gather | bytes 860160 | tf_op jit(solution)/shard_map/all_gather | solution.py:61
  230.6 13.9 %all_gather.34 = bf16[7,384,128]{2,1,0:T(8,128)(2,1)S(1)} all-gather(bf16[7,96,128]{2,1,0:T(8,128)(2,1)S(1)} %collective-permute-done.11), channel_id=1, replica_groups=mesh['dom'=128,'field'=4] {'field'}, dimensions={1}, use_global_device_ids=true | all-gather | bytes 860160 | tf_op jit(solution)/shard_map/all_gather | solution.py:61
  256.5 14.0 %all_gather.35 = bf16[8,384,128]{2,1,0:T(8,128)(2,1)} all-gather(bf16[8,96,128]{2,1,0:T(8,128)(2,1)S(1)} %fusion.7), channel_id=1, replica_groups=mesh['dom'=128,'field'=4] {'field'}, dimensions={1}, use_global_device_ids=true | all-gather | bytes 983040 | tf_op jit(solution)/shard_map/all_gather | solution.py:55
  284.7 3.6 collective-permute-start.13
  288.4 6.2 %collective-permute-start.14 = (bf16[7,96,128]{2,1,0:T(8,128)(2,1)S(1)}, bf16[7,96,128]{2,1,0:T(8,128)(2,1)S(1)}, u32[]{:S(2)}, u32[]{:S(2)}) collective-permute-start(bf16[7,96,128]{2,1,0:T(8,128)(2,1)S(1)} %broadcast_select_fusion.4), channel_id=1, source_target_pairs={{0,64},{4,68},{8,72},{12,76},{16,80},{20,84},{24,88},{28,92},{32,9... | collective-permute-start | bytes 516104 | tf_op jit(solution)/shard_map/ppermute | solution.py:12
  294.8 8.3 %collective-permute-start.15 = (bf16[7,96,128]{2,1,0:T(8,128)(2,1)S(1)}, bf16[7,96,128]{2,1,0:T(8,128)(2,1)S(1)}, u32[]{:S(2)}, u32[]{:S(2)}) collective-permute-start(bf16[7,96,128]{2,1,0:T(8,128)(2,1)S(1)} %broadcast_select_fusion.2), channel_id=1, source_target_pairs={{0,448},{4,452},{8,456},{12,460},{16,464},{20,468},{24,472},{28,47... | collective-permute-start | bytes 516104 | tf_op jit(solution)/shard_map/ppermute | solution.py:12
  304.4 12.6 %collective-permute-done.12 = bf16[7,96,128]{2,1,0:T(8,128)(2,1)S(1)} collective-permute-done((bf16[7,96,128]{2,1,0:T(8,128)(2,1)S(1)}, bf16[7,96,128]{2,1,0:T(8,128)(2,1)S(1)}, u32[]{:S(2)}, u32[]{:S(2)}) %collective-permute-start.12) | collective-permute-done | bytes 172064 | tf_op jit(solution)/shard_map/ppermute | solution.py:12
  317.1 13.1 %all_gather.36 = bf16[7,384,128]{2,1,0:T(8,128)(2,1)S(1)} all-gather(bf16[7,96,128]{2,1,0:T(8,128)(2,1)S(1)} %collective-permute-done.12), channel_id=1, replica_groups=mesh['dom'=128,'field'=4] {'field'}, dimensions={1}, use_global_device_ids=true | all-gather | bytes 860160 | tf_op jit(solution)/shard_map/all_gather | solution.py:61
  330.2 14.2 %all_gather.37 = bf16[7,384,128]{2,1,0:T(8,128)(2,1)S(1)} all-gather(bf16[7,96,128]{2,1,0:T(8,128)(2,1)S(1)} %collective-permute-done.13), channel_id=1, replica_groups=mesh['dom'=128,'field'=4] {'field'}, dimensions={1}, use_global_device_ids=true | all-gather | bytes 860160 | tf_op jit(solution)/shard_map/all_gather | solution.py:61
  344.5 13.1 %all_gather.38 = bf16[7,384,128]{2,1,0:T(8,128)(2,1)S(1)} all-gather(bf16[7,96,128]{2,1,0:T(8,128)(2,1)S(1)} %collective-permute-done.14), channel_id=1, replica_groups=mesh['dom'=128,'field'=4] {'field'}, dimensions={1}, use_global_device_ids=true | all-gather | bytes 860160 | tf_op jit(solution)/shard_map/all_gather | solution.py:61
  357.8 13.1 %all_gather.39 = bf16[7,384,128]{2,1,0:T(8,128)(2,1)S(1)} all-gather(bf16[7,96,128]{2,1,0:T(8,128)(2,1)S(1)} %collective-permute-done.15), channel_id=1, replica_groups=mesh['dom'=128,'field'=4] {'field'}, dimensions={1}, use_global_device_ids=true | all-gather | bytes 860160 | tf_op jit(solution)/shard_map/all_gather | solution.py:61
  (101 shorter events, 64.6 us)
Async XLA Ops:
  0.6 254.8 %copy-start = (bf16[8,96,384]{2,1,0:T(8,128)(2,1)S(1)}, bf16[8,96,384]{2,1,0:T(8,128)(2,1)}, u32[]{:S(2)}) copy-start(bf16[8,96,384]{2,1,0:T(8,128)(2,1)} %param.13) | copy-start | bytes 1769476
  0.6 4.4 %copy-start.15 = (s32[35]{0:T(128)S(1)}, s32[35]{0:T(128)}, u32[]{:S(2)}) copy-start(s32[35]{0:T(128)} %param.16) | copy-start | bytes 424
  31.5 4.1 %copy-start.16 = (s32[1,5]{1,0:T(1,128)S(1)}, s32[1,5]{1,0:T(1,128)}, u32[]{:S(2)}) copy-start(s32[1,5]{1,0:T(1,128)} %param.17) | copy-start | bytes 64
  36.1 13.2 %copy-start.7 = (s32[35]{0:T(128)S(1)}, s32[35]{0:T(128)}, u32[]{:S(2)}) copy-start(s32[35]{0:T(128)} %param.14) | copy-start | bytes 424
  36.2 13.9 %copy-start.3 = (bf16[8,96,128]{2,1,0:T(8,128)(2,1)S(1)}, bf16[8,96,128]{2,1,0:T(8,128)(2,1)}, u32[]{:S(2)}) copy-start(bf16[8,96,128]{2,1,0:T(8,128)(2,1)} %param.11) | copy-start | bytes 589828
  36.2 17.2 %copy-start.6 = (s32[35]{0:T(128)S(1)}, s32[35]{0:T(128)}, u32[]{:S(2)}) copy-start(s32[35]{0:T(128)} %param.15) | copy-start | bytes 424
  37.6 210.5 %collective-permute-start.4 = (bf16[7,96,384]{2,1,0:T(8,128)(2,1)}, bf16[7,96,384]{2,1,0:T(8,128)(2,1)}, u32[]{:S(2)}, u32[]{:S(2)}) collective-permute-start(bf16[7,96,384]{2,1,0:T(8,128)(2,1)} %get-tuple-element.17), channel_id=1, source_target_pairs={{0,4},{4,8},{8,12},{12,16},{16,20},{20,24},{24,28},{28,32},{32,36}... | collective-permute-start | bytes 1548296 | tf_op jit(solution)/shard_map/ppermute | solution.py:12
  39.6 209.8 %collective-permute-start.5 = (bf16[7,96,384]{2,1,0:T(8,128)(2,1)}, bf16[7,96,384]{2,1,0:T(8,128)(2,1)}, u32[]{:S(2)}, u32[]{:S(2)}) collective-permute-start(bf16[7,96,384]{2,1,0:T(8,128)(2,1)} %get-tuple-element.16), channel_id=1, source_target_pairs={{0,508},{4,0},{8,4},{12,8},{16,12},{20,16},{24,20},{28,24},{32,28}... | collective-permute-start | bytes 1548296 | tf_op jit(solution)/shard_map/ppermute | solution.py:12
  43.2 207.3 %collective-permute-start.6 = (bf16[7,96,384]{2,1,0:T(8,128)(2,1)}, bf16[7,96,384]{2,1,0:T(8,128)(2,1)}, u32[]{:S(2)}, u32[]{:S(2)}) collective-permute-start(bf16[7,96,384]{2,1,0:T(8,128)(2,1)} %get-tuple-element.15), channel_id=1, source_target_pairs={{0,64},{4,68},{8,72},{12,76},{16,80},{20,84},{24,88},{28,92},{32,9... | collective-permute-start | bytes 1548296 | tf_op jit(solution)/shard_map/ppermute | solution.py:12
  50.0 23.7 %copy-start.13 = (pred[7]{0:T(512)(128)(4,1)}, pred[7]{0:T(512)(128)(4,1)S(1)}, u32[]{:S(2)}) copy-start(pred[7]{0:T(512)(128)(4,1)S(1)} %get-tuple-element.26) | copy-start | bytes 25
  51.4 85.8 %collective-permute-start.8 = (bf16[7,96,128]{2,1,0:T(8,128)(2,1)}, bf16[7,96,128]{2,1,0:T(8,128)(2,1)}, u32[]{:S(2)}, u32[]{:S(2)}) collective-permute-start(bf16[7,96,128]{2,1,0:T(8,128)(2,1)} %broadcast_select_fusion.9), channel_id=1, source_target_pairs={{0,4},{4,8},{8,12},{12,16},{16,20},{20,24},{24,28},{28,32},{32,36}... | collective-permute-start | bytes 516104 | tf_op jit(solution)/shard_map/ppermute | solution.py:12
  54.0 36.7 %collective-permute-start = (s32[7]{0:T(128)}, s32[7]{0:T(128)}, u32[]{:S(2)}, u32[]{:S(2)}) collective-permute-start(s32[7]{0:T(128)} %get-tuple-element.21), channel_id=1, source_target_pairs={{0,4},{4,8},{8,12},{12,16},{16,20},{20,24},{24,28},{28,32},{32,36}... | collective-permute-start | bytes 92 | tf_op jit(solution)/shard_map/ppermute | solution.py:12
  90.7 7.6 %collective-permute-start.1 = (s32[7]{0:T(128)}, s32[7]{0:T(128)}, u32[]{:S(2)}, u32[]{:S(2)}) collective-permute-start(s32[7]{0:T(128)} %get-tuple-element.20), channel_id=1, source_target_pairs={{0,508},{4,0},{8,4},{12,8},{16,12},{20,16},{24,20},{28,24},{32,28}... | collective-permute-start | bytes 92 | tf_op jit(solution)/shard_map/ppermute | solution.py:12
  98.3 14.2 %collective-permute-start.2 = (s32[7]{0:T(128)}, s32[7]{0:T(128)}, u32[]{:S(2)}, u32[]{:S(2)}) collective-permute-start(s32[7]{0:T(128)} %get-tuple-element.23), channel_id=1, source_target_pairs={{0,64},{4,68},{8,72},{12,76},{16,80},{20,84},{24,88},{28,92},{32,9... | collective-permute-start | bytes 92 | tf_op jit(solution)/shard_map/ppermute | solution.py:12
  112.5 15.2 %collective-permute-start.3 = (s32[7]{0:T(128)}, s32[7]{0:T(128)}, u32[]{:S(2)}, u32[]{:S(2)}) collective-permute-start(s32[7]{0:T(128)} %get-tuple-element.19), channel_id=1, source_target_pairs={{0,448},{4,452},{8,456},{12,460},{16,464},{20,468},{24,472},{28,47... | collective-permute-start | bytes 92 | tf_op jit(solution)/shard_map/ppermute | solution.py:12
  127.7 124.0 %collective-permute-start.7 = (bf16[7,96,384]{2,1,0:T(8,128)(2,1)}, bf16[7,96,384]{2,1,0:T(8,128)(2,1)}, u32[]{:S(2)}, u32[]{:S(2)}) collective-permute-start(bf16[7,96,384]{2,1,0:T(8,128)(2,1)} %get-tuple-element.14), channel_id=1, source_target_pairs={{0,448},{4,452},{8,456},{12,460},{16,464},{20,468},{24,472},{28,47... | collective-permute-start | bytes 1548296 | tf_op jit(solution)/shard_map/ppermute | solution.py:12
  137.2 51.5 %collective-permute-start.9 = (bf16[7,96,128]{2,1,0:T(8,128)(2,1)}, bf16[7,96,128]{2,1,0:T(8,128)(2,1)S(1)}, u32[]{:S(2)}, u32[]{:S(2)}) collective-permute-start(bf16[7,96,128]{2,1,0:T(8,128)(2,1)} %broadcast_select_fusion.7), channel_id=1, source_target_pairs={{0,508},{4,0},{8,4},{12,8},{16,12},{20,16},{24,20},{28,24},{32,28}... | collective-permute-start | bytes 516104 | tf_op jit(solution)/shard_map/ppermute | solution.py:12
  188.7 19.2 %collective-permute-start.10 = (bf16[7,96,128]{2,1,0:T(8,128)(2,1)}, bf16[7,96,128]{2,1,0:T(8,128)(2,1)S(1)}, u32[]{:S(2)}, u32[]{:S(2)}) collective-permute-start(bf16[7,96,128]{2,1,0:T(8,128)(2,1)} %broadcast_select_fusion.5), channel_id=1, source_target_pairs={{0,64},{4,68},{8,72},{12,76},{16,80},{20,84},{24,88},{28,92},{32,9... | collective-permute-start | bytes 516104 | tf_op jit(solution)/shard_map/ppermute | solution.py:12
  208.0 22.7 %collective-permute-start.11 = (bf16[7,96,128]{2,1,0:T(8,128)(2,1)S(1)}, bf16[7,96,128]{2,1,0:T(8,128)(2,1)S(1)}, u32[]{:S(2)}, u32[]{:S(2)}) collective-permute-start(bf16[7,96,128]{2,1,0:T(8,128)(2,1)S(1)} %broadcast_select_fusion.3), channel_id=1, source_target_pairs={{0,448},{4,452},{8,456},{12,460},{16,464},{20,468},{24,472},{28,47... | collective-permute-start | bytes 516104 | tf_op jit(solution)/shard_map/ppermute | solution.py:12
  248.1 4.7 %copy-start.5 = (bf16[35,384,128]{2,1,0:T(8,128)(2,1)S(1)}, bf16[35,384,128]{2,1,0:T(8,128)(2,1)}, u32[]{:S(2)}) copy-start(bf16[35,384,128]{2,1,0:T(8,128)(2,1)} %constant_dynamic-update-slice_fusion.4) | copy-start | bytes 10321924
  252.8 0.9 copy-start.9
  253.7 1.7 copy-start.1
  255.5 25.3 %copy-start.14 = (pred[7]{0:T(512)(128)(4,1)S(1)}, pred[7]{0:T(512)(128)(4,1)}, u32[]{:S(2)}) copy-start(pred[7]{0:T(512)(128)(4,1)} %copy-done.13) | copy-start | bytes 25
  256.5 27.2 %copy-start.12 = (pred[7]{0:T(512)(128)(4,1)S(1)}, pred[7]{0:T(512)(128)(4,1)}, u32[]{:S(2)}) copy-start(pred[7]{0:T(512)(128)(4,1)} %get-tuple-element.24) | copy-start | bytes 25
  256.5 31.8 %copy-start.11 = (pred[7]{0:T(512)(128)(4,1)S(1)}, pred[7]{0:T(512)(128)(4,1)}, u32[]{:S(2)}) copy-start(pred[7]{0:T(512)(128)(4,1)} %get-tuple-element.30) | copy-start | bytes 25
  256.5 38.2 %copy-start.10 = (pred[7]{0:T(512)(128)(4,1)S(1)}, pred[7]{0:T(512)(128)(4,1)}, u32[]{:S(2)}) copy-start(pred[7]{0:T(512)(128)(4,1)} %get-tuple-element.4) | copy-start | bytes 25
  256.5 46.6 %copy-start.8 = (pred[7]{0:T(512)(128)(4,1)S(1)}, pred[7]{0:T(512)(128)(4,1)}, u32[]{:S(2)}) copy-start(pred[7]{0:T(512)(128)(4,1)} %get-tuple-element.28) | copy-start | bytes 25
  281.7 35.3 %collective-permute-start.12 = (bf16[7,96,128]{2,1,0:T(8,128)(2,1)S(1)}, bf16[7,96,128]{2,1,0:T(8,128)(2,1)S(1)}, u32[]{:S(2)}, u32[]{:S(2)}) collective-permute-start(bf16[7,96,128]{2,1,0:T(8,128)(2,1)S(1)} %broadcast_select_fusion.8), channel_id=1, source_target_pairs={{0,4},{4,8},{8,12},{12,16},{16,20},{20,24},{24,28},{28,32},{32,36}... | collective-permute-start | bytes 516104 | tf_op jit(solution)/shard_map/ppermute | solution.py:12
  284.7 45.5 %collective-permute-start.13 = (bf16[7,96,128]{2,1,0:T(8,128)(2,1)S(1)}, bf16[7,96,128]{2,1,0:T(8,128)(2,1)S(1)}, u32[]{:S(2)}, u32[]{:S(2)}) collective-permute-start(bf16[7,96,128]{2,1,0:T(8,128)(2,1)S(1)} %broadcast_select_fusion.6), channel_id=1, source_target_pairs={{0,508},{4,0},{8,4},{12,8},{16,12},{20,16},{24,20},{28,24},{32,28}... | collective-permute-start | bytes 516104 | tf_op jit(solution)/shard_map/ppermute | solution.py:12
  288.4 56.1 %collective-permute-start.14 = (bf16[7,96,128]{2,1,0:T(8,128)(2,1)S(1)}, bf16[7,96,128]{2,1,0:T(8,128)(2,1)S(1)}, u32[]{:S(2)}, u32[]{:S(2)}) collective-permute-start(bf16[7,96,128]{2,1,0:T(8,128)(2,1)S(1)} %broadcast_select_fusion.4), channel_id=1, source_target_pairs={{0,64},{4,68},{8,72},{12,76},{16,80},{20,84},{24,88},{28,92},{32,9... | collective-permute-start | bytes 516104 | tf_op jit(solution)/shard_map/ppermute | solution.py:12
  294.8 63.0 %collective-permute-start.15 = (bf16[7,96,128]{2,1,0:T(8,128)(2,1)S(1)}, bf16[7,96,128]{2,1,0:T(8,128)(2,1)S(1)}, u32[]{:S(2)}, u32[]{:S(2)}) collective-permute-start(bf16[7,96,128]{2,1,0:T(8,128)(2,1)S(1)} %broadcast_select_fusion.2), channel_id=1, source_target_pairs={{0,448},{4,452},{8,456},{12,460},{16,464},{20,468},{24,472},{28,47... | collective-permute-start | bytes 516104 | tf_op jit(solution)/shard_map/ppermute | solution.py:12
  371.9 1.7 copy-start.2
  (1 other events, 0.7 us)
where the time goes:
time: 377 us; the launch traced here: 375 us
  blocking collectives  138 us (37%)
  starting transfers between devices  78.8 us (21%)
  waiting for transfers between devices  71.4 us (19%)
  local copies, waits for them, and re-layouts  53 us (14%)
  other arithmetic  25.6 us (7%)
  matrix products  6.55 us (2%)
    all_gather x8, blocking collectives, apply_op(): row_list.append(lax.all_gather(landed, 'field', axis=1, tiled=True))  109 us
    ppermute x16, starting transfers between devices, from_behind(): lax.ppermute(array, axis, [(i, (i + by) % peers) for i in range(peers)])  78.8 us
    ppermute x16, waiting for transfers between devices, from_behind(): lax.ppermute(array, axis, [(i, (i + by) % peers) for i in range(peers)])  71.4 us
    all_gather x2, blocking collectives, apply_op(): whole = lax.all_gather(vector, 'field', axis=1, tiled=True)  29.1 us
    rev x1, local copies, waits for them, and re-layouts, orient(): shaped = jnp.where(flip_cols, jnp.flip(shaped, 3), shaped)  15 us
    gather x8, local copies, waits for them, and re-layouts, apply_op(): halo_rows = jnp.take(vector, sources[side], axis=0)  11.2 us
  transfers between devices with their start and end apart: 16, of which 7 were waited for; matrix products, arithmetic and copies ran while one was open for 8% of the time, Pallas kernels for 0%

commit v1 on v0

--- a/solution.py
+++ b/solution.py
@@ -58,7 +58,12 @@
         for side in range(1, NS):
             halo_rows = jnp.take(vector, sources[side], axis=0)
             landed = from_behind(halo_rows, "dom", offsets[side])
-            row_list.append(lax.all_gather(landed, "field", axis=1, tiled=True))
+            row_list.append(
+                jnp.concatenate(
+                    lax.all_to_all(jnp.stack([landed] * lax.axis_size("field")), "field", 0, 0),
+                    axis=1,
+                )
+            )
         rows_all = jnp.concatenate(row_list, 0)
         product = jnp.einsum(
             "scr,srk->sck", all_blocks, rows_all, preferred_element_type=jnp.float32

time: 377 us -> 423 us (1.12)
  the two profiles are of different devices: /device:TPU:466 before, /device:TPU:24 now
where the time goes in v1:
time: 423 us; the launch traced here: 420 us
  waiting for transfers between devices  145 us (34%)
  starting transfers between devices  117 us (28%)
  local copies, waits for them, and re-layouts  77.8 us (18%)
  blocking collectives  43.1 us (10%)
  other arithmetic  24.5 us (6%)
  matrix products  11.2 us (3%)
    ppermute x16, waiting for transfers between devices, from_behind(): lax.ppermute(array, axis, [(i, (i + by) % peers) for i in range(peers)])  142 us
    ppermute x16, starting transfers between devices, from_behind(): lax.ppermute(array, axis, [(i, (i + by) % peers) for i in range(peers)])  80.7 us
    all_gather x2, blocking collectives, apply_op(): whole = lax.all_gather(vector, 'field', axis=1, tiled=True)  43.1 us
    all_to_all x8, starting transfers between devices, apply_op(): lax.all_to_all(jnp.stack([landed] * lax.axis_size('field')), 'field', 0, 0)  36.2 us
    rev x1, local copies, waits for them, and re-layouts, orient(): shaped = jnp.where(flip_cols, jnp.flip(shaped, 3), shaped)  15.1 us
    reshape x8, local copies, waits for them, and re-layouts, apply_op(): jnp.concatenate(lax.all_to_all(jnp.stack([landed] * lax.axis_size('field'...  14.7 us
    unnamed x55, local copies, waits for them, and re-layouts  11 us
    another operation x8, local copies, waits for them, and re-layouts, apply_op(): jnp.stack([landed] * lax.axis_size('field'))  9.57 us
  transfers between devices with their start and end apart: 24, of which 9 were waited for; matrix products, arithmetic and copies ran while one was open for 19% of the time, Pallas kernels for 0%

profile of v1, /device:TPU:24, one launch (start us, length us, event | category | flops | bytes accessed | tf_op | source)
XLA Modules:
  0.0 419.9 jit_solution(5023224799269471578)
XLA Ops:
  7.9 11.1 %collective-permute-start.9 = (bf16[7,96,128]{2,1,0:T(8,128)(2,1)}, bf16[7,96,128]{2,1,0:T(8,128)(2,1)}, u32[]{:S(2)}, u32[]{:S(2)}) collective-permute-start(bf16[7,96,128]{2,1,0:T(8,128)(2,1)} %broadcast_select_fusion.7), channel_id=1, source_target_pairs={{0,508},{4,0},{8,4},{12,8},{16,12},{20,16},{24,20},{28,24},{32,28}... | collective-permute-start | bytes 516104 | tf_op jit(solution)/shard_map/ppermute | solution.py:12
  19.1 4.3 %reshape.136 = bf16[35,6,4,4,384]{4,3,2,1,0:T(4,128)(2,1)S(1)} reshape(bf16[35,96,384]{2,1,0:T(8,128)(2,1)} %param.12) | data formatting | bytes 5160960 | tf_op jit(solution)/shard_map/reshape | solution.py:17
  26.6 15.1 %rev.9 = bf16[35,6,4,4,384]{4,3,2,1,0:T(4,128)(2,1)} reverse(bf16[35,6,4,4,384]{4,3,2,1,0:T(4,128)(2,1)} %reverse_select_fusion), dimensions={3} | reverse | bytes 5160960 | tf_op jit(solution)/shard_map/jit(_flip)/rev | solution.py:22
  41.7 5.2 %broadcast_select_fusion = bf16[35,6,4,4,384]{4,3,2,1,0:T(4,128)(2,1)S(1)} fusion(bf16[35,6,4,4,384]{4,3,2,1,0:T(4,128)(2,1)} %rev.9, pred[35]{0:T(512)(128)(4,1)S(1)} %get-tuple-element.34, bf16[35,6,4,4,384]{4,3,2,1,0:T(4,128)(2,1)S(1)} %reshape.136, pred[35]{0:T(512)(128)(4,1)S(1)} %get-tuple-element.33), kind=kLoop, calls=%fused_computation.12 | loop fusion | flops 2580480 | bytes 7741510 | tf_op jit(solution)/shard_map/jit(_where)/select_n | solution.py:22
  50.0 4.1 reshape.137
  55.2 4.3 %all-to-all-start = ((bf16[4,7,96,128]{3,2,1,0:T(8,128)(2,1)}), bf16[4,7,96,128]{3,2,1,0:T(8,128)(2,1)}, u32[]{:S(2)}, u32[]{:S(2)}) async-start(bf16[4,7,96,128]{3,2,1,0:T(8,128)(2,1)} %stack.16), calls=%async_computation | async-start | bytes 1376256 | tf_op jit(solution)/shard_map/all_to_all | solution.py:63
  63.2 5.8 %collective-permute-start.5 = (bf16[7,96,384]{2,1,0:T(8,128)(2,1)}, bf16[7,96,384]{2,1,0:T(8,128)(2,1)}, u32[]{:S(2)}, u32[]{:S(2)}) collective-permute-start(bf16[7,96,384]{2,1,0:T(8,128)(2,1)} %get-tuple-element.16), channel_id=1, source_target_pairs={{0,508},{4,0},{8,4},{12,8},{16,12},{20,16},{24,20},{28,24},{32,28}... | collective-permute-start | bytes 1548296 | tf_op jit(solution)/shard_map/ppermute | solution.py:12
  68.9 8.7 %collective-permute-start.6 = (bf16[7,96,384]{2,1,0:T(8,128)(2,1)}, bf16[7,96,384]{2,1,0:T(8,128)(2,1)}, u32[]{:S(2)}, u32[]{:S(2)}) collective-permute-start(bf16[7,96,384]{2,1,0:T(8,128)(2,1)} %get-tuple-element.15), channel_id=1, source_target_pairs={{0,64},{4,68},{8,72},{12,76},{16,80},{20,84},{24,88},{28,92},{32,9... | collective-permute-start | bytes 1548296 | tf_op jit(solution)/shard_map/ppermute | solution.py:12
  77.6 6.8 %collective-permute-start.7 = (bf16[7,96,384]{2,1,0:T(8,128)(2,1)}, bf16[7,96,384]{2,1,0:T(8,128)(2,1)}, u32[]{:S(2)}, u32[]{:S(2)}) collective-permute-start(bf16[7,96,384]{2,1,0:T(8,128)(2,1)} %get-tuple-element.14), channel_id=1, source_target_pairs={{0,448},{4,452},{8,456},{12,460},{16,464},{20,468},{24,472},{28,47... | collective-permute-start | bytes 1548296 | tf_op jit(solution)/shard_map/ppermute | solution.py:12
  86.9 4.9 %all-to-all-start.1 = ((bf16[4,7,96,128]{3,2,1,0:T(8,128)(2,1)}), bf16[4,7,96,128]{3,2,1,0:T(8,128)(2,1)}, u32[]{:S(2)}, u32[]{:S(2)}) async-start(bf16[4,7,96,128]{3,2,1,0:T(8,128)(2,1)} %stack.17), calls=%async_computation.1 | async-start | bytes 1376256 | tf_op jit(solution)/shard_map/all_to_all | solution.py:63
  93.2 7.7 %collective-permute-start.10 = (bf16[7,96,128]{2,1,0:T(8,128)(2,1)}, bf16[7,96,128]{2,1,0:T(8,128)(2,1)}, u32[]{:S(2)}, u32[]{:S(2)}) collective-permute-start(bf16[7,96,128]{2,1,0:T(8,128)(2,1)} %broadcast_select_fusion.5), channel_id=1, source_target_pairs={{0,64},{4,68},{8,72},{12,76},{16,80},{20,84},{24,88},{28,92},{32,9... | collective-permute-start | bytes 516104 | tf_op jit(solution)/shard_map/ppermute | solution.py:12
  104.2 79.7 %collective-permute-done.10 = bf16[7,96,128]{2,1,0:T(8,128)(2,1)} collective-permute-done((bf16[7,96,128]{2,1,0:T(8,128)(2,1)}, bf16[7,96,128]{2,1,0:T(8,128)(2,1)}, u32[]{:S(2)}, u32[]{:S(2)}) %collective-permute-start.10) | collective-permute-done | bytes 172064 | tf_op jit(solution)/shard_map/ppermute | solution.py:12
  183.9 8.0 %collective-permute-start.11 = (bf16[7,96,128]{2,1,0:T(8,128)(2,1)}, bf16[7,96,128]{2,1,0:T(8,128)(2,1)S(1)}, u32[]{:S(2)}, u32[]{:S(2)}) collective-permute-start(bf16[7,96,128]{2,1,0:T(8,128)(2,1)} %broadcast_select_fusion.3), channel_id=1, source_target_pairs={{0,448},{4,452},{8,456},{12,460},{16,464},{20,468},{24,472},{28,47... | collective-permute-start | bytes 516104 | tf_op jit(solution)/shard_map/ppermute | solution.py:12
  193.9 4.8 %all-to-all-start.2 = ((bf16[4,7,96,128]{3,2,1,0:T(8,128)(2,1)}), bf16[4,7,96,128]{3,2,1,0:T(8,128)(2,1)}, u32[]{:S(2)}, u32[]{:S(2)}) async-start(bf16[4,7,96,128]{3,2,1,0:T(8,128)(2,1)} %stack.18), calls=%async_computation.2 | async-start | bytes 1376256 | tf_op jit(solution)/shard_map/all_to_all | solution.py:63
  198.7 21.4 %all_gather.6 = bf16[8,384,128]{2,1,0:T(8,128)(2,1)} all-gather(bf16[8,96,128]{2,1,0:T(8,128)(2,1)S(1)} %copy-done.3), channel_id=1, replica_groups=mesh['dom'=128,'field'=4] {'field'}, dimensions={1}, use_global_device_ids=true | all-gather | bytes 983040 | tf_op jit(solution)/shard_map/all_gather | solution.py:55
  226.9 4.5 %all-to-all-start.3 = ((bf16[4,7,96,128]{3,2,1,0:T(8,128)(2,1)}), bf16[4,7,96,128]{3,2,1,0:T(8,128)(2,1)}, u32[]{:S(2)}, u32[]{:S(2)}) async-start(bf16[4,7,96,128]{3,2,1,0:T(8,128)(2,1)} %stack.19), calls=%async_computation.3 | async-start | bytes 1376256 | tf_op jit(solution)/shard_map/all_to_all | solution.py:63
  233.6 5.7 %collective-permute-start.1 = (s32[7]{0:T(128)S(1)}, s32[7]{0:T(128)S(1)}, u32[]{:S(2)}, u32[]{:S(2)}) collective-permute-start(s32[7]{0:T(128)S(1)} %copy-done.20), channel_id=1, source_target_pairs={{0,508},{4,0},{8,4},{12,8},{16,12},{20,16},{24,20},{28,24},{32,28}... | collective-permute-start | bytes 92 | tf_op jit(solution)/shard_map/ppermute | solution.py:12
  240.6 3.2 collective-permute-start.2
  243.9 11.8 %collective-permute-done.2 = s32[7]{0:T(128)S(1)} collective-permute-done((s32[7]{0:T(128)S(1)}, s32[7]{0:T(128)S(1)}, u32[]{:S(2)}, u32[]{:S(2)}) %collective-permute-start.2) | collective-permute-done | bytes 60 | tf_op jit(solution)/shard_map/ppermute | solution.py:12
  255.7 4.0 collective-permute-start.3
  259.7 10.1 %collective-permute-done.3 = s32[7]{0:T(128)S(1)} collective-permute-done((s32[7]{0:T(128)S(1)}, s32[7]{0:T(128)S(1)}, u32[]{:S(2)}, u32[]{:S(2)}) %collective-permute-start.3) | collective-permute-done | bytes 60 | tf_op jit(solution)/shard_map/ppermute | solution.py:12
  297.0 6.9 %collective-permute-done.12 = bf16[7,96,128]{2,1,0:T(8,128)(2,1)S(1)} collective-permute-done((bf16[7,96,128]{2,1,0:T(8,128)(2,1)S(1)}, bf16[7,96,128]{2,1,0:T(8,128)(2,1)S(1)}, u32[]{:S(2)}, u32[]{:S(2)}) %collective-permute-start.12) | collective-permute-done | bytes 172064 | tf_op jit(solution)/shard_map/ppermute | solution.py:12
  304.9 4.5 %all-to-all-start.4 = ((bf16[4,7,96,128]{3,2,1,0:T(8,128)(2,1)}), bf16[4,7,96,128]{3,2,1,0:T(8,128)(2,1)}, u32[]{:S(2)}, u32[]{:S(2)}) async-start(bf16[4,7,96,128]{3,2,1,0:T(8,128)(2,1)} %stack.20), calls=%async_computation.4 | async-start | bytes 1376256 | tf_op jit(solution)/shard_map/all_to_all | solution.py:63
  314.9 3.5 all-to-all-done.4
  319.4 4.2 all-to-all-start.5
  324.9 4.2 collective-permute-start.14
  329.0 16.1 %collective-permute-done.14 = bf16[7,96,128]{2,1,0:T(8,128)(2,1)S(1)} collective-permute-done((bf16[7,96,128]{2,1,0:T(8,128)(2,1)S(1)}, bf16[7,96,128]{2,1,0:T(8,128)(2,1)S(1)}, u32[]{:S(2)}, u32[]{:S(2)}) %collective-permute-start.14) | collective-permute-done | bytes 172064 | tf_op jit(solution)/shard_map/ppermute | solution.py:12
  346.1 4.5 %all-to-all-start.6 = ((bf16[4,7,96,128]{3,2,1,0:T(8,128)(2,1)}), bf16[4,7,96,128]{3,2,1,0:T(8,128)(2,1)}, u32[]{:S(2)}, u32[]{:S(2)}) async-start(bf16[4,7,96,128]{3,2,1,0:T(8,128)(2,1)} %stack.22), calls=%async_computation.6 | async-start | bytes 1376256 | tf_op jit(solution)/shard_map/all_to_all | solution.py:63
  351.6 5.8 %collective-permute-start.15 = (bf16[7,96,128]{2,1,0:T(8,128)(2,1)S(1)}, bf16[7,96,128]{2,1,0:T(8,128)(2,1)S(1)}, u32[]{:S(2)}, u32[]{:S(2)}) collective-permute-start(bf16[7,96,128]{2,1,0:T(8,128)(2,1)S(1)} %broadcast_select_fusion.2), channel_id=1, source_target_pairs={{0,448},{4,452},{8,456},{12,460},{16,464},{20,468},{24,472},{28,47... | collective-permute-start | bytes 516104 | tf_op jit(solution)/shard_map/ppermute | solution.py:12
  357.4 12.7 %collective-permute-done.15 = bf16[7,96,128]{2,1,0:T(8,128)(2,1)S(1)} collective-permute-done((bf16[7,96,128]{2,1,0:T(8,128)(2,1)S(1)}, bf16[7,96,128]{2,1,0:T(8,128)(2,1)S(1)}, u32[]{:S(2)}, u32[]{:S(2)}) %collective-permute-start.15) | collective-permute-done | bytes 172064 | tf_op jit(solution)/shard_map/ppermute | solution.py:12
  371.1 4.5 %all-to-all-start.7 = ((bf16[4,7,96,128]{3,2,1,0:T(8,128)(2,1)}), bf16[4,7,96,128]{3,2,1,0:T(8,128)(2,1)}, u32[]{:S(2)}, u32[]{:S(2)}) async-start(bf16[4,7,96,128]{3,2,1,0:T(8,128)(2,1)} %stack.23), calls=%async_computation.7 | async-start | bytes 1376256 | tf_op jit(solution)/shard_map/all_to_all | solution.py:63
  375.6 21.7 %all_gather.7 = bf16[8,384,128]{2,1,0:T(8,128)(2,1)} all-gather(bf16[8,96,128]{2,1,0:T(8,128)(2,1)S(1)} %copy-done.4), channel_id=1, replica_groups=mesh['dom'=128,'field'=4] {'field'}, dimensions={1}, use_global_device_ids=true | all-gather | bytes 983040 | tf_op jit(solution)/shard_map/all_gather | solution.py:55
  (137 shorter events, 98.7 us)
Async XLA Ops:
  0.6 291.1 %copy-start = (bf16[8,96,384]{2,1,0:T(8,128)(2,1)S(1)}, bf16[8,96,384]{2,1,0:T(8,128)(2,1)}, u32[]{:S(2)}) copy-start(bf16[8,96,384]{2,1,0:T(8,128)(2,1)} %param.13) | copy-start | bytes 1769476
  2.1 21.3 %copy-start.16 = (pred[7]{0:T(512)(128)(4,1)}, pred[7]{0:T(512)(128)(4,1)S(1)}, u32[]{:S(2)}) copy-start(pred[7]{0:T(512)(128)(4,1)S(1)} %get-tuple-element.26) | copy-start | bytes 25
  3.7 50.5 %collective-permute-start.8 = (bf16[7,96,128]{2,1,0:T(8,128)(2,1)S(1)}, bf16[7,96,128]{2,1,0:T(8,128)(2,1)S(1)}, u32[]{:S(2)}, u32[]{:S(2)}) collective-permute-start(bf16[7,96,128]{2,1,0:T(8,128)(2,1)S(1)} %broadcast_select_fusion.9), channel_id=1, source_target_pairs={{0,4},{4,8},{8,12},{12,16},{16,20},{20,24},{24,28},{28,32},{32,36}... | collective-permute-start | bytes 516104 | tf_op jit(solution)/shard_map/ppermute | solution.py:12
  7.9 77.1 %collective-permute-start.9 = (bf16[7,96,128]{2,1,0:T(8,128)(2,1)}, bf16[7,96,128]{2,1,0:T(8,128)(2,1)}, u32[]{:S(2)}, u32[]{:S(2)}) collective-permute-start(bf16[7,96,128]{2,1,0:T(8,128)(2,1)} %broadcast_select_fusion.7), channel_id=1, source_target_pairs={{0,508},{4,0},{8,4},{12,8},{16,12},{20,16},{24,20},{28,24},{32,28}... | collective-permute-start | bytes 516104 | tf_op jit(solution)/shard_map/ppermute | solution.py:12
  55.2 29.8 %all-to-all-start = ((bf16[4,7,96,128]{3,2,1,0:T(8,128)(2,1)}), bf16[4,7,96,128]{3,2,1,0:T(8,128)(2,1)}, u32[]{:S(2)}, u32[]{:S(2)}) async-start(bf16[4,7,96,128]{3,2,1,0:T(8,128)(2,1)} %stack.16), calls=%async_computation | async-start | bytes 1376256 | tf_op jit(solution)/shard_map/all_to_all | solution.py:63
  59.8 24.6 %copy-start.3 = (bf16[8,96,128]{2,1,0:T(8,128)(2,1)S(1)}, bf16[8,96,128]{2,1,0:T(8,128)(2,1)}, u32[]{:S(2)}) copy-start(bf16[8,96,128]{2,1,0:T(8,128)(2,1)} %param.11) | copy-start | bytes 589828
  61.3 209.3 %collective-permute-start.4 = (bf16[7,96,384]{2,1,0:T(8,128)(2,1)}, bf16[7,96,384]{2,1,0:T(8,128)(2,1)}, u32[]{:S(2)}, u32[]{:S(2)}) collective-permute-start(bf16[7,96,384]{2,1,0:T(8,128)(2,1)} %get-tuple-element.17), channel_id=1, source_target_pairs={{0,4},{4,8},{8,12},{12,16},{16,20},{20,24},{24,28},{28,32},{32,36}... | collective-permute-start | bytes 1548296 | tf_op jit(solution)/shard_map/ppermute | solution.py:12
  63.2 208.5 %collective-permute-start.5 = (bf16[7,96,384]{2,1,0:T(8,128)(2,1)}, bf16[7,96,384]{2,1,0:T(8,128)(2,1)}, u32[]{:S(2)}, u32[]{:S(2)}) collective-permute-start(bf16[7,96,384]{2,1,0:T(8,128)(2,1)} %get-tuple-element.16), channel_id=1, source_target_pairs={{0,508},{4,0},{8,4},{12,8},{16,12},{20,16},{24,20},{28,24},{32,28}... | collective-permute-start | bytes 1548296 | tf_op jit(solution)/shard_map/ppermute | solution.py:12
  68.9 203.9 %collective-permute-start.6 = (bf16[7,96,384]{2,1,0:T(8,128)(2,1)}, bf16[7,96,384]{2,1,0:T(8,128)(2,1)}, u32[]{:S(2)}, u32[]{:S(2)}) collective-permute-start(bf16[7,96,384]{2,1,0:T(8,128)(2,1)} %get-tuple-element.15), channel_id=1, source_target_pairs={{0,64},{4,68},{8,72},{12,76},{16,80},{20,84},{24,88},{28,92},{32,9... | collective-permute-start | bytes 1548296 | tf_op jit(solution)/shard_map/ppermute | solution.py:12
  77.6 196.4 %collective-permute-start.7 = (bf16[7,96,384]{2,1,0:T(8,128)(2,1)}, bf16[7,96,384]{2,1,0:T(8,128)(2,1)}, u32[]{:S(2)}, u32[]{:S(2)}) collective-permute-start(bf16[7,96,384]{2,1,0:T(8,128)(2,1)} %get-tuple-element.14), channel_id=1, source_target_pairs={{0,448},{4,452},{8,456},{12,460},{16,464},{20,468},{24,472},{28,47... | collective-permute-start | bytes 1548296 | tf_op jit(solution)/shard_map/ppermute | solution.py:12
  86.9 133.2 %copy-start.9 = (s32[35]{0:T(128)S(1)}, s32[35]{0:T(128)}, u32[]{:S(2)}) copy-start(s32[35]{0:T(128)} %param.15) | copy-start | bytes 424
  86.9 105.0 %all-to-all-start.1 = ((bf16[4,7,96,128]{3,2,1,0:T(8,128)(2,1)}), bf16[4,7,96,128]{3,2,1,0:T(8,128)(2,1)}, u32[]{:S(2)}, u32[]{:S(2)}) async-start(bf16[4,7,96,128]{3,2,1,0:T(8,128)(2,1)} %stack.17), calls=%async_computation.1 | async-start | bytes 1376256 | tf_op jit(solution)/shard_map/all_to_all | solution.py:63
  93.2 90.7 %collective-permute-start.10 = (bf16[7,96,128]{2,1,0:T(8,128)(2,1)}, bf16[7,96,128]{2,1,0:T(8,128)(2,1)}, u32[]{:S(2)}, u32[]{:S(2)}) collective-permute-start(bf16[7,96,128]{2,1,0:T(8,128)(2,1)} %broadcast_select_fusion.5), channel_id=1, source_target_pairs={{0,64},{4,68},{8,72},{12,76},{16,80},{20,84},{24,88},{28,92},{32,9... | collective-permute-start | bytes 516104 | tf_op jit(solution)/shard_map/ppermute | solution.py:12
  183.9 40.1 %collective-permute-start.11 = (bf16[7,96,128]{2,1,0:T(8,128)(2,1)}, bf16[7,96,128]{2,1,0:T(8,128)(2,1)S(1)}, u32[]{:S(2)}, u32[]{:S(2)}) collective-permute-start(bf16[7,96,128]{2,1,0:T(8,128)(2,1)} %broadcast_select_fusion.3), channel_id=1, source_target_pairs={{0,448},{4,452},{8,456},{12,460},{16,464},{20,468},{24,472},{28,47... | collective-permute-start | bytes 516104 | tf_op jit(solution)/shard_map/ppermute | solution.py:12
  193.9 32.0 %all-to-all-start.2 = ((bf16[4,7,96,128]{3,2,1,0:T(8,128)(2,1)}), bf16[4,7,96,128]{3,2,1,0:T(8,128)(2,1)}, u32[]{:S(2)}, u32[]{:S(2)}) async-start(bf16[4,7,96,128]{3,2,1,0:T(8,128)(2,1)} %stack.18), calls=%async_computation.2 | async-start | bytes 1376256 | tf_op jit(solution)/shard_map/all_to_all | solution.py:63
  224.0 9.6 %collective-permute-start = (s32[7]{0:T(128)}, s32[7]{0:T(128)}, u32[]{:S(2)}, u32[]{:S(2)}) collective-permute-start(s32[7]{0:T(128)} %get-tuple-element.21), channel_id=1, source_target_pairs={{0,4},{4,8},{8,12},{12,16},{16,20},{20,24},{24,28},{28,32},{32,36}... | collective-permute-start | bytes 92 | tf_op jit(solution)/shard_map/ppermute | solution.py:12
  226.9 28.8 %copy-start.18 = (s32[7]{0:T(128)S(1)}, s32[7]{0:T(128)}, u32[]{:S(2)}) copy-start(s32[7]{0:T(128)} %get-tuple-element.19) | copy-start | bytes 88
  226.9 43.0 %copy-start.17 = (s32[7]{0:T(128)S(1)}, s32[7]{0:T(128)}, u32[]{:S(2)}) copy-start(s32[7]{0:T(128)} %get-tuple-element.22) | copy-start | bytes 88
  226.9 54.3 %all-to-all-start.3 = ((bf16[4,7,96,128]{3,2,1,0:T(8,128)(2,1)}), bf16[4,7,96,128]{3,2,1,0:T(8,128)(2,1)}, u32[]{:S(2)}, u32[]{:S(2)}) async-start(bf16[4,7,96,128]{3,2,1,0:T(8,128)(2,1)} %stack.19), calls=%async_computation.3 | async-start | bytes 1376256 | tf_op jit(solution)/shard_map/all_to_all | solution.py:63
  233.6 7.0 %collective-permute-start.1 = (s32[7]{0:T(128)S(1)}, s32[7]{0:T(128)S(1)}, u32[]{:S(2)}, u32[]{:S(2)}) collective-permute-start(s32[7]{0:T(128)S(1)} %copy-done.20), channel_id=1, source_target_pairs={{0,508},{4,0},{8,4},{12,8},{16,12},{20,16},{24,20},{28,24},{32,28}... | collective-permute-start | bytes 92 | tf_op jit(solution)/shard_map/ppermute | solution.py:12
  240.6 15.1 %collective-permute-start.2 = (s32[7]{0:T(128)S(1)}, s32[7]{0:T(128)S(1)}, u32[]{:S(2)}, u32[]{:S(2)}) collective-permute-start(s32[7]{0:T(128)S(1)} %copy-done.19), channel_id=1, source_target_pairs={{0,64},{4,68},{8,72},{12,76},{16,80},{20,84},{24,88},{28,92},{32,9... | collective-permute-start | bytes 92 | tf_op jit(solution)/shard_map/ppermute | solution.py:12
  255.7 14.2 %collective-permute-start.3 = (s32[7]{0:T(128)S(1)}, s32[7]{0:T(128)S(1)}, u32[]{:S(2)}, u32[]{:S(2)}) collective-permute-start(s32[7]{0:T(128)S(1)} %copy-done.18), channel_id=1, source_target_pairs={{0,448},{4,452},{8,456},{12,460},{16,464},{20,468},{24,472},{28,47... | collective-permute-start | bytes 92 | tf_op jit(solution)/shard_map/ppermute | solution.py:12
  295.1 8.8 %collective-permute-start.12 = (bf16[7,96,128]{2,1,0:T(8,128)(2,1)S(1)}, bf16[7,96,128]{2,1,0:T(8,128)(2,1)S(1)}, u32[]{:S(2)}, u32[]{:S(2)}) collective-permute-start(bf16[7,96,128]{2,1,0:T(8,128)(2,1)S(1)} %broadcast_select_fusion.8), channel_id=1, source_target_pairs={{0,4},{4,8},{8,12},{12,16},{16,20},{20,24},{24,28},{28,32},{32,36}... | collective-permute-start | bytes 516104 | tf_op jit(solution)/shard_map/ppermute | solution.py:12
  304.9 13.5 %all-to-all-start.4 = ((bf16[4,7,96,128]{3,2,1,0:T(8,128)(2,1)}), bf16[4,7,96,128]{3,2,1,0:T(8,128)(2,1)}, u32[]{:S(2)}, u32[]{:S(2)}) async-start(bf16[4,7,96,128]{3,2,1,0:T(8,128)(2,1)} %stack.20), calls=%async_computation.4 | async-start | bytes 1376256 | tf_op jit(solution)/shard_map/all_to_all | solution.py:63
  310.0 41.4 %copy-start.13 = (pred[7]{0:T(512)(128)(4,1)S(1)}, pred[7]{0:T(512)(128)(4,1)}, u32[]{:S(2)}) copy-start(pred[7]{0:T(512)(128)(4,1)} %get-tuple-element.4) | copy-start | bytes 25
  310.1 4.8 %collective-permute-start.13 = (bf16[7,96,128]{2,1,0:T(8,128)(2,1)S(1)}, bf16[7,96,128]{2,1,0:T(8,128)(2,1)S(1)}, u32[]{:S(2)}, u32[]{:S(2)}) collective-permute-start(bf16[7,96,128]{2,1,0:T(8,128)(2,1)S(1)} %broadcast_select_fusion.6), channel_id=1, source_target_pairs={{0,508},{4,0},{8,4},{12,8},{16,12},{20,16},{24,20},{28,24},{32,28}... | collective-permute-start | bytes 516104 | tf_op jit(solution)/shard_map/ppermute | solution.py:12
  319.4 25.8 %all-to-all-start.5 = ((bf16[4,7,96,128]{3,2,1,0:T(8,128)(2,1)}), bf16[4,7,96,128]{3,2,1,0:T(8,128)(2,1)}, u32[]{:S(2)}, u32[]{:S(2)}) async-start(bf16[4,7,96,128]{3,2,1,0:T(8,128)(2,1)} %stack.21), calls=%async_computation.5 | async-start | bytes 1376256 | tf_op jit(solution)/shard_map/all_to_all | solution.py:63
  324.9 20.3 %collective-permute-start.14 = (bf16[7,96,128]{2,1,0:T(8,128)(2,1)S(1)}, bf16[7,96,128]{2,1,0:T(8,128)(2,1)S(1)}, u32[]{:S(2)}, u32[]{:S(2)}) collective-permute-start(bf16[7,96,128]{2,1,0:T(8,128)(2,1)S(1)} %broadcast_select_fusion.4), channel_id=1, source_target_pairs={{0,64},{4,68},{8,72},{12,76},{16,80},{20,84},{24,88},{28,92},{32,9... | collective-permute-start | bytes 516104 | tf_op jit(solution)/shard_map/ppermute | solution.py:12
  346.1 24.0 %all-to-all-start.6 = ((bf16[4,7,96,128]{3,2,1,0:T(8,128)(2,1)}), bf16[4,7,96,128]{3,2,1,0:T(8,128)(2,1)}, u32[]{:S(2)}, u32[]{:S(2)}) async-start(bf16[4,7,96,128]{3,2,1,0:T(8,128)(2,1)} %stack.22), calls=%async_computation.6 | async-start | bytes 1376256 | tf_op jit(solution)/shard_map/all_to_all | solution.py:63
  350.6 49.4 %copy-start.10 = (pred[7]{0:T(512)(128)(4,1)S(1)}, pred[7]{0:T(512)(128)(4,1)}, u32[]{:S(2)}) copy-start(pred[7]{0:T(512)(128)(4,1)} %get-tuple-element.28) | copy-start | bytes 25
  351.6 18.5 %collective-permute-start.15 = (bf16[7,96,128]{2,1,0:T(8,128)(2,1)S(1)}, bf16[7,96,128]{2,1,0:T(8,128)(2,1)S(1)}, u32[]{:S(2)}, u32[]{:S(2)}) collective-permute-start(bf16[7,96,128]{2,1,0:T(8,128)(2,1)S(1)} %broadcast_select_fusion.2), channel_id=1, source_target_pairs={{0,448},{4,452},{8,456},{12,460},{16,464},{20,468},{24,472},{28,47... | collective-permute-start | bytes 516104 | tf_op jit(solution)/shard_map/ppermute | solution.py:12
  371.1 37.2 %all-to-all-start.7 = ((bf16[4,7,96,128]{3,2,1,0:T(8,128)(2,1)}), bf16[4,7,96,128]{3,2,1,0:T(8,128)(2,1)}, u32[]{:S(2)}, u32[]{:S(2)}) async-start(bf16[4,7,96,128]{3,2,1,0:T(8,128)(2,1)} %stack.23), calls=%async_computation.7 | async-start | bytes 1376256 | tf_op jit(solution)/shard_map/all_to_all | solution.py:63
  (15 other events, 134.1 us)
